TPU v7x, 32 devices: a whole 2x2x4 slice. The times are simulated.
32 devices in a mesh: view: 4 (over x, core), samp: 8 (over z, y).
Axes of the slice: x: 2, y: 2, z: 4, core: 2. Of those that a mesh axis runs over, the one named last changes fastest.
Arguments:
- view_data: bfloat16 [8, 4096, 2048], P('view', 'samp'), may hold values from -10 to 10
- init_coeffs: float32 [8, 2048, 128], P('view'), may hold values from -0.125 to 0.125
Outputs:
- shared_scores: float32 [4096, 128], P('samp')
- final_coeffs: float32 [8, 2048, 128], P('view', 'samp')
All inputs are finite; a program needn't handle non-finite values.
Results may differ from a plain program's by a relative error of at most 0.005.
Values may be sent and summed in bfloat16 or wider, within the bound.
No kernel may reach another device: no remote copies, remote signals or barrier semaphores. Data moves between devices by JAX's collectives and lax.ppermute only.
A program may use at most 128 MiB of HBM per device.

v0:
```python
import jax
import jax.numpy as jnp
from jax import lax
from jax.sharding import PartitionSpec as P

OUTER = 2
INNER = 2
NS_ITERS = 12
HIGH = lax.Precision.HIGHEST
ridge_weight = 0.1
step_size = 0.5


def newton_inverse(gram):
    size_k = gram.shape[0]
    eye_mat = jnp.eye(size_k, dtype=jnp.float32)
    shrunk = gram + jnp.trace(gram) / size_k * eye_mat
    scale = jnp.sqrt(jnp.sum(shrunk * shrunk))
    approx = shrunk / scale
    inverse = eye_mat
    for turn in range(NS_ITERS):
        factor = 0.5 * (3.0 * eye_mat - jnp.dot(inverse, approx, precision=HIGH))
        approx = jnp.dot(approx, factor, precision=HIGH)
        inverse = jnp.dot(factor, inverse, precision=HIGH)
    return (inverse, scale)


def make_scores(view_data, coeffs_low, total):
    local_sum = jnp.zeros((view_data.shape[1], coeffs_low.shape[2]), jnp.float32)
    for member in range(view_data.shape[0]):
        local_sum = local_sum + jnp.dot(
            view_data[member], coeffs_low[member], preferred_element_type=jnp.float32
        )
    summed = lax.psum(local_sum, "view")
    gram = lax.psum(jnp.dot(summed.T, summed, precision=HIGH), "samp")
    inverse, scale = newton_inverse(gram)
    return jnp.dot(summed, inverse, precision=HIGH) * jnp.sqrt(total / scale)


def grad_term(samples, weights_low, scores):
    resid = (jnp.dot(samples, weights_low, preferred_element_type=jnp.float32) - scores).astype(
        jnp.bfloat16
    )
    return lax.dot_general(
        samples, resid, (((0,), (0,)), ((), ())), preferred_element_type=jnp.float32
    )


def body(view_data, init_coeffs):
    total = view_data.shape[1] * lax.axis_size("samp")
    row_count = init_coeffs.shape[1] // lax.axis_size("samp")
    row_start = lax.axis_index("samp") * row_count
    own_coeffs = lax.dynamic_slice_in_dim(init_coeffs, row_start, row_count, 1)
    coeffs_low = init_coeffs.astype(jnp.bfloat16)
    scores = make_scores(view_data, coeffs_low, total)
    for outer_step in range(OUTER):
        for inner_step in range(INNER):
            terms = jnp.stack(
                [
                    grad_term(view_data[member], coeffs_low[member], scores)
                    for member in range(view_data.shape[0])
                ]
            )
            summed_grad = lax.psum_scatter(terms, "samp", scatter_dimension=1, tiled=True)
            own_coeffs = own_coeffs - step_size * (summed_grad / total + ridge_weight * own_coeffs)
            coeffs_low = lax.all_gather(own_coeffs.astype(jnp.bfloat16), "samp", axis=1, tiled=True)
        scores = make_scores(view_data, coeffs_low, total)
    return (scores, own_coeffs)


def solution(mesh):
    in_specs = (P("view", "samp", None), P("view", None, None))
    out_specs = (P("samp", None), P("view", "samp", None))
    return jax.shard_map(body, mesh=mesh, in_specs=in_specs, out_specs=out_specs, check_vma=False)
```

profile of v0, /device:TPU:0, one launch (start us, length us, event | category | flops | bytes accessed | tf_op | source)
XLA Modules:
  0.0 856.1 jit_solution(11644975215844309981)
XLA Ops:
  7.2 1.9 convert_element_type.42
  9.1 2.3 fusion.12
  11.4 1.4 fusion.163
  12.9 35.1 %all-reduce.7.cloned.1.call-done = f32[512,128]{1,0:T(8,128)} async-done(((f32[512,128]{1,0:T(8,128)}), f32[512,128]{1,0:T(8,128)}) %all-reduce.7.cloned.1.call-update) | async-done | bytes 262160 | tf_op jit(solution)/shard_map/psum | solution.py:34
  48.0 2.2 fusion.165
  50.4 70.9 %all-reduce.9.cloned.1.call-done = f32[128,128]{1,0:T(8,128)} async-done(((f32[128,128]{1,0:T(8,128)}), f32[128,128]{1,0:T(8,128)}) %all-reduce.9.cloned.1.call-update) | async-done | bytes 65552 | tf_op jit(solution)/shard_map/psum | solution.py:35
  121.3 1.5 select_reduce_fusion.2
  123.4 1.5 multiply_reduce_fusion.2
  126.8 1.1 fusion.152
  135.1 2.3 convolution_bitcast_fusion.6
  138.0 1.5 pad_maximum_fusion
  140.7 67.8 %reduce-scatter.5.cloned.1.call-done = f32[2,256,128]{1,2,0:T(8,128)} async-done(((f32[2,2048,128]{1,2,0:T(8,128)}), f32[2,256,128]{1,2,0:T(8,128)}) %reduce-scatter.5.cloned.1.call-update) | async-done | bytes 262160 | tf_op jit(solution)/shard_map/reduce_scatter | solution.py:64
  208.5 1.7 fusion.144
  210.3 39.2 %all-gather.5.cloned.1.call-done = bf16[2,2048,128]{1,2,0:T(8,128)(2,1)} async-done(((bf16[2,256,128]{1,2,0:T(8,128)(2,1)}), bf16[2,2048,128]{1,2,0:T(8,128)(2,1)}) %all-gather.5.cloned.1.call-update) | async-done | bytes 1048592 | tf_op jit(solution)/shard_map/all_gather | solution.py:66
  249.5 4.0 convolution_bitcast_fusion.4
  253.4 4.0 convolution_bitcast_fusion.5
  257.4 1.5 pad_maximum_fusion.1
  259.0 68.0 %reduce-scatter.7.cloned.1.call-done = f32[2,256,128]{1,2,0:T(8,128)} async-done(((f32[2,2048,128]{1,2,0:T(8,128)}), f32[2,256,128]{1,2,0:T(8,128)}) %reduce-scatter.7.cloned.1.call-update) | async-done | bytes 262160 | tf_op jit(solution)/shard_map/reduce_scatter | solution.py:64
  327.0 1.7 fusion.162
  328.7 39.1 %all-gather.7.cloned.1.call-done = bf16[2,2048,128]{1,2,0:T(8,128)(2,1)} async-done(((bf16[2,256,128]{1,2,0:T(8,128)(2,1)}), bf16[2,2048,128]{1,2,0:T(8,128)(2,1)}) %all-gather.7.cloned.1.call-update) | async-done | bytes 1048592 | tf_op jit(solution)/shard_map/all_gather | solution.py:66
  367.9 2.7 fusion.55
  370.6 3.1 fusion.164
  374.0 31.2 %all-reduce.11.cloned.1.call-done = f32[512,128]{0,1:T(8,128)} async-done(((f32[512,128]{0,1:T(8,128)}), f32[512,128]{0,1:T(8,128)}) %all-reduce.11.cloned.1.call-update) | async-done | bytes 262160 | tf_op jit(solution)/shard_map/psum | solution.py:34
  405.2 2.0 fusion.187
  407.3 71.1 %all-reduce.13.cloned.1.call-done = f32[128,128]{1,0:T(8,128)} async-done(((f32[128,128]{1,0:T(8,128)}), f32[128,128]{1,0:T(8,128)}) %all-reduce.13.cloned.1.call-update) | async-done | bytes 65552 | tf_op jit(solution)/shard_map/psum | solution.py:35
  478.4 1.5 select_reduce_fusion.1
  480.6 1.5 multiply_reduce_fusion.1
  484.0 1.1 fusion.149
  492.3 2.3 convolution_bitcast_fusion.2
  495.2 1.5 pad_maximum_fusion.2
  496.7 69.1 %reduce-scatter.9.cloned.1.call-done = f32[2,256,128]{1,2,0:T(8,128)} async-done(((f32[2,2048,128]{1,2,0:T(8,128)}), f32[2,256,128]{1,2,0:T(8,128)}) %reduce-scatter.9.cloned.1.call-update) | async-done | bytes 262160 | tf_op jit(solution)/shard_map/reduce_scatter | solution.py:64
  565.8 1.7 fusion.145
  567.5 39.2 %all-gather.9.cloned.1.call-done = bf16[2,2048,128]{1,2,0:T(8,128)(2,1)} async-done(((bf16[2,256,128]{1,2,0:T(8,128)(2,1)}), bf16[2,2048,128]{1,2,0:T(8,128)(2,1)}) %all-gather.9.cloned.1.call-update) | async-done | bytes 1048592 | tf_op jit(solution)/shard_map/all_gather | solution.py:66
  606.7 3.6 convolution_bitcast_fusion
  610.3 3.6 convolution_bitcast_fusion.1
  613.9 1.5 pad_maximum_fusion.3
  615.5 68.0 %reduce-scatter.11.cloned.1.call-done = f32[2,256,128]{1,2,0:T(8,128)} async-done(((f32[2,2048,128]{1,2,0:T(8,128)}), f32[2,256,128]{1,2,0:T(8,128)}) %reduce-scatter.11.cloned.1.call-update) | async-done | bytes 262160 | tf_op jit(solution)/shard_map/reduce_scatter | solution.py:64
  683.5 1.7 fusion.161
  685.3 39.1 %all-gather.11.cloned.1.call-done = bf16[2,2048,128]{1,2,0:T(8,128)(2,1)} async-done(((bf16[2,256,128]{1,2,0:T(8,128)(2,1)}), bf16[2,2048,128]{1,2,0:T(8,128)(2,1)}) %all-gather.11.cloned.1.call-update) | async-done | bytes 1048592 | tf_op jit(solution)/shard_map/all_gather | solution.py:66
  724.4 2.7 fusion
  727.1 3.1 fusion.46
  730.5 31.2 %all-reduce.15.cloned.1.call-done = f32[512,128]{0,1:T(8,128)} async-done(((f32[512,128]{0,1:T(8,128)}), f32[512,128]{0,1:T(8,128)}) %all-reduce.15.cloned.1.call-update) | async-done | bytes 262160 | tf_op jit(solution)/shard_map/psum | solution.py:34
  761.7 2.0 fusion.209
  764.6 70.2 %all-reduce.17.cloned.1.call-done = f32[128,128]{1,0:T(8,128)} async-done(((f32[128,128]{1,0:T(8,128)}), f32[128,128]{1,0:T(8,128)}) %all-reduce.17.cloned.1.call-update) | async-done | bytes 65552 | tf_op jit(solution)/shard_map/psum | solution.py:35
  834.8 1.5 select_reduce_fusion
  837.0 1.5 multiply_reduce_fusion
  840.4 1.1 fusion.146
  848.3 1.3 convolution_multiply_fusion
  (157 shorter events, 28.4 us)
Async XLA Ops:
  7.2 40.9 %all-reduce.7.cloned.1.call-start = ((), (), s32[]{:S(2)}) async-start(), calls=%async_computation.4 | async-start | bytes 524288 | tf_op jit(solution)/shard_map/psum | solution.py:34
  7.2 4.2 copy-start
  12.9 108.4 %all-reduce.9.cloned.1.call-start = ((), (), s32[]{:S(2)}) async-start(), calls=%async_computation.5 | async-start | bytes 131072 | tf_op jit(solution)/shard_map/psum | solution.py:35
  50.3 158.2 %reduce-scatter.5.cloned.1.call-start = ((), (), s32[]{:S(2)}) async-start(), calls=%async_computation.6 | async-start | bytes 2359296 | tf_op jit(solution)/shard_map/reduce_scatter | solution.py:64
  130.2 4.5 copy-start.4
  134.7 2.8 copy-start.1
  139.6 109.9 %all-gather.5.cloned.1.call-start = ((), (), s32[]{:S(2)}) async-start(), calls=%async_computation.7 | async-start | bytes 1179648 | tf_op jit(solution)/shard_map/all_gather | solution.py:66
  210.2 116.8 %reduce-scatter.7.cloned.1.call-start = ((), (), s32[]{:S(2)}) async-start(), calls=%async_computation.8 | async-start | bytes 2359296 | tf_op jit(solution)/shard_map/reduce_scatter | solution.py:64
  258.9 68.1 %copy-start.6 = (f32[2,256,128]{1,2,0:T(8,128)S(1)}, f32[2,256,128]{1,2,0:T(8,128)}, u32[]{:S(2)}) copy-start(f32[2,256,128]{1,2,0:T(8,128)} %reduce-scatter.5.cloned.1.call-done) | copy-start | bytes 786436
  258.9 109.0 %all-gather.7.cloned.1.call-start = ((), (), s32[]{:S(2)}) async-start(), calls=%async_computation.9 | async-start | bytes 1179648 | tf_op jit(solution)/shard_map/all_gather | solution.py:66
  328.7 76.5 %all-reduce.11.cloned.1.call-start = ((), (), s32[]{:S(2)}) async-start(), calls=%async_computation.10 | async-start | bytes 524288 | tf_op jit(solution)/shard_map/psum | solution.py:34
  367.9 2.7 copy-start.8
  373.7 104.7 %all-reduce.13.cloned.1.call-start = ((), (), s32[]{:S(2)}) async-start(), calls=%async_computation.11 | async-start | bytes 131072 | tf_op jit(solution)/shard_map/psum | solution.py:35
  407.3 158.5 %reduce-scatter.9.cloned.1.call-start = ((), (), s32[]{:S(2)}) async-start(), calls=%async_computation.12 | async-start | bytes 2359296 | tf_op jit(solution)/shard_map/reduce_scatter | solution.py:64
  487.4 4.5 copy-start.5
  491.9 2.8 copy-start.2
  496.7 110.0 %all-gather.9.cloned.1.call-start = ((), (), s32[]{:S(2)}) async-start(), calls=%async_computation.13 | async-start | bytes 1179648 | tf_op jit(solution)/shard_map/all_gather | solution.py:66
  567.5 116.0 %reduce-scatter.11.cloned.1.call-start = ((), (), s32[]{:S(2)}) async-start(), calls=%async_computation.14 | async-start | bytes 2359296 | tf_op jit(solution)/shard_map/reduce_scatter | solution.py:64
  615.4 68.1 %copy-start.7 = (f32[2,256,128]{1,2,0:T(8,128)S(1)}, f32[2,256,128]{1,2,0:T(8,128)}, u32[]{:S(2)}) copy-start(f32[2,256,128]{1,2,0:T(8,128)} %reduce-scatter.9.cloned.1.call-done) | copy-start | bytes 786436
  615.4 109.0 %all-gather.11.cloned.1.call-start = ((), (), s32[]{:S(2)}) async-start(), calls=%async_computation.15 | async-start | bytes 1179648 | tf_op jit(solution)/shard_map/all_gather | solution.py:66
  685.2 76.5 %all-reduce.15.cloned.1.call-start = ((), (), s32[]{:S(2)}) async-start(), calls=%async_computation.16 | async-start | bytes 524288 | tf_op jit(solution)/shard_map/psum | solution.py:34
  724.4 2.7 copy-start.9
  730.3 104.6 %all-reduce.17.cloned.1.call-start = ((), (), s32[]{:S(2)}) async-start(), calls=%async_computation.17 | async-start | bytes 131072 | tf_op jit(solution)/shard_map/psum | solution.py:35
  843.8 4.5 copy-start.3
Sparse Core Ops, SparseCore 0:
  13.0 35.0 all-reduce.6
  52.0 69.2 all-reduce.8
  139.7 68.8 reduce-scatter.4
  211.0 38.3 all-gather.4
  259.0 67.8 reduce-scatter.6
  329.4 38.4 all-gather.6
  373.9 31.2 all-reduce.10
  409.2 69.2 all-reduce.12
  496.8 68.9 reduce-scatter.8
  568.2 38.3 all-gather.8
  615.6 67.9 reduce-scatter.10
  686.0 38.3 all-gather.10
  730.4 31.2 all-reduce.14
  765.6 69.2 all-reduce.16
where the time goes:
time: 857 us; the launch traced here: 856 us
  waiting for transfers between devices  740 us (86%)
  matrix products  70.7 us (8%)
  other arithmetic  23.3 us (3%)
  between operations  19.3 us (2%)
    reduce_scatter x4, waiting for transfers between devices, body(): lax.psum_scatter(terms, 'samp', scatter_dimension=1, tiled=True)  273 us
    psum x3, waiting for transfers between devices, make_scores(): gram = lax.psum(jnp.dot(summed.T, summed, precision=HIGH), 'samp')  212 us
    all_gather x4, waiting for transfers between devices, body(): lax.all_gather(own_coeffs.astype(jnp.bfloat16), 'samp', axis=1, tiled=True)  157 us
    psum x3, waiting for transfers between devices, make_scores(): summed = lax.psum(local_sum, 'view')  97.5 us
    dot_general x8, matrix products, grad_term(): lax.dot_general(samples, resid, (((0,), (0,)), ((), ())), preferred_eleme...  20.6 us
  transfers between devices with their start and end apart: 14, of which 14 were waited for; matrix products, arithmetic and copies ran while one was open for 0% of the time, Pallas kernels for 0%

commit v1 on v0

--- a/solution.py
+++ b/solution.py
@@ -31,7 +31,22 @@
         local_sum = local_sum + jnp.dot(
             view_data[member], coeffs_low[member], preferred_element_type=jnp.float32
         )
-    summed = lax.psum(local_sum, "view")
+
+    def tell_unit(panel):
+        devs = lax.axis_size("view")
+
+        def words_remake(far_arr, right_arr):
+            if right_arr >= devs:
+                return far_arr
+            return words_remake(
+                far_arr
+                + lax.ppermute(far_arr, "view", [(i0, i0 ^ right_arr) for i0 in range(devs)]),
+                2 * right_arr,
+            )
+
+        return words_remake(panel, 1)
+
+    summed = tell_unit(local_sum)
     gram = lax.psum(jnp.dot(summed.T, summed, precision=HIGH), "samp")
     inverse, scale = newton_inverse(gram)
     return jnp.dot(summed, inverse, precision=HIGH) * jnp.sqrt(total / scale)

time: 857 us -> 781 us (0.911)
  waiting for transfers between devices: 740 us -> 661 us
    psum x3 -> x0, waiting for transfers between devices: 97.5 us -> none  [make_scores(): summed = lax.psum(local_sum, 'view')]
    ppermute x0 -> x6, waiting for transfers between devices: none -> 24.3 us  [words_remake(): lax.ppermute(far_arr, 'view', [(i0, i0 ^ right_arr) for i0 in range(devs)])]
  transfers between devices with their start and end apart: 14 -> 17, of which waited for: 14 -> 17; matrix products, arithmetic and copies ran while one was open for 0% -> 0% of each run, Pallas kernels for 0% -> 0%
where the time goes in v1:
time: 781 us; the launch traced here: 780 us
  waiting for transfers between devices  661 us (85%)
  matrix products  65.4 us (8%)
  other arithmetic  23.5 us (3%)
  between operations  19.2 us (2%)
    reduce_scatter x4, waiting for transfers between devices, body(): lax.psum_scatter(terms, 'samp', scatter_dimension=1, tiled=True)  274 us
    psum x3, waiting for transfers between devices, make_scores(): gram = lax.psum(jnp.dot(summed.T, summed, precision=HIGH), 'samp')  207 us
    all_gather x4, waiting for transfers between devices, body(): lax.all_gather(own_coeffs.astype(jnp.bfloat16), 'samp', axis=1, tiled=True)  157 us
    ppermute x6, waiting for transfers between devices, words_remake(): lax.ppermute(far_arr, 'view', [(i0, i0 ^ right_arr) for i0 in range(devs)])  24.3 us
    dot_general x8, matrix products, grad_term(): lax.dot_general(samples, resid, (((0,), (0,)), ((), ())), preferred_eleme...  20.6 us
  transfers between devices with their start and end apart: 17, of which 17 were waited for; matrix products, arithmetic and copies ran while one was open for 0% of the time, Pallas kernels for 0%

profile of v1, /device:TPU:0, one launch (start us, length us, event | category | flops | bytes accessed | tf_op | source)
XLA Modules:
  0.0 779.6 jit_solution(14524889822174105532)
XLA Ops:
  7.2 1.9 convert_element_type.42
  9.1 2.3 fusion.12
  12.7 1.2 collective-permute-done
  13.9 2.9 collective-permute-start.1
  16.8 6.6 collective-permute-done.1
  23.5 1.2 fusion.165
  24.7 70.9 %all-reduce.4.cloned.1.call-done = f32[128,128]{1,0:T(8,128)} async-done(((f32[128,128]{1,0:T(8,128)}), f32[128,128]{1,0:T(8,128)}) %all-reduce.4.cloned.1.call-update) | async-done | bytes 65552 | tf_op jit(solution)/shard_map/psum | solution.py:50
  95.6 1.5 select_reduce_fusion.2
  97.7 1.5 multiply_reduce_fusion.2
  109.4 2.3 convolution_bitcast_fusion.6
  112.3 1.5 pad_maximum_fusion
  115.0 68.1 %reduce-scatter.5.cloned.1.call-done = f32[2,256,128]{1,2,0:T(8,128)} async-done(((f32[2,2048,128]{1,2,0:T(8,128)}), f32[2,256,128]{1,2,0:T(8,128)}) %reduce-scatter.5.cloned.1.call-update) | async-done | bytes 262160 | tf_op jit(solution)/shard_map/reduce_scatter | solution.py:79
  183.1 1.7 fusion.144
  184.8 39.4 %all-gather.5.cloned.1.call-done = bf16[2,2048,128]{1,2,0:T(8,128)(2,1)} async-done(((bf16[2,256,128]{1,2,0:T(8,128)(2,1)}), bf16[2,2048,128]{1,2,0:T(8,128)(2,1)}) %all-gather.5.cloned.1.call-update) | async-done | bytes 1048592 | tf_op jit(solution)/shard_map/all_gather | solution.py:81
  224.2 4.0 convolution_bitcast_fusion.4
  228.2 4.0 convolution_bitcast_fusion.5
  232.1 1.5 pad_maximum_fusion.1
  233.7 68.3 %reduce-scatter.7.cloned.1.call-done = f32[2,256,128]{1,2,0:T(8,128)} async-done(((f32[2,2048,128]{1,2,0:T(8,128)}), f32[2,256,128]{1,2,0:T(8,128)}) %reduce-scatter.7.cloned.1.call-update) | async-done | bytes 262160 | tf_op jit(solution)/shard_map/reduce_scatter | solution.py:79
  302.0 1.7 fusion.162
  303.9 38.9 %all-gather.7.cloned.1.call-done = bf16[2,2048,128]{1,2,0:T(8,128)(2,1)} async-done(((bf16[2,256,128]{1,2,0:T(8,128)(2,1)}), bf16[2,2048,128]{1,2,0:T(8,128)(2,1)}) %all-gather.7.cloned.1.call-update) | async-done | bytes 1048592 | tf_op jit(solution)/shard_map/all_gather | solution.py:81
  342.9 2.7 fusion.55
  345.6 2.4 fusion.164
  348.1 1.5 collective-permute-done.2
  349.6 1.7 collective-permute-start.3
  351.3 6.8 collective-permute-done.3
  359.2 68.4 %all-reduce.6.cloned.1.call-done = f32[128,128]{1,0:T(8,128)} async-done(((f32[128,128]{1,0:T(8,128)}), f32[128,128]{1,0:T(8,128)}) %all-reduce.6.cloned.1.call-update) | async-done | bytes 65552 | tf_op jit(solution)/shard_map/psum | solution.py:50
  427.5 1.5 select_reduce_fusion.1
  429.6 1.5 multiply_reduce_fusion.1
  441.4 2.3 convolution_bitcast_fusion.2
  444.2 1.5 pad_maximum_fusion.2
  445.8 68.8 %reduce-scatter.9.cloned.1.call-done = f32[2,256,128]{1,2,0:T(8,128)} async-done(((f32[2,2048,128]{1,2,0:T(8,128)}), f32[2,256,128]{1,2,0:T(8,128)}) %reduce-scatter.9.cloned.1.call-update) | async-done | bytes 262160 | tf_op jit(solution)/shard_map/reduce_scatter | solution.py:79
  514.6 1.7 fusion.145
  516.3 39.3 %all-gather.9.cloned.1.call-done = bf16[2,2048,128]{1,2,0:T(8,128)(2,1)} async-done(((bf16[2,256,128]{1,2,0:T(8,128)(2,1)}), bf16[2,2048,128]{1,2,0:T(8,128)(2,1)}) %all-gather.9.cloned.1.call-update) | async-done | bytes 1048592 | tf_op jit(solution)/shard_map/all_gather | solution.py:81
  555.7 3.6 convolution_bitcast_fusion
  559.3 3.6 convolution_bitcast_fusion.1
  562.9 1.5 pad_maximum_fusion.3
  564.4 68.4 %reduce-scatter.11.cloned.1.call-done = f32[2,256,128]{1,2,0:T(8,128)} async-done(((f32[2,2048,128]{1,2,0:T(8,128)}), f32[2,256,128]{1,2,0:T(8,128)}) %reduce-scatter.11.cloned.1.call-update) | async-done | bytes 262160 | tf_op jit(solution)/shard_map/reduce_scatter | solution.py:79
  632.8 1.7 fusion.161
  634.8 38.9 %all-gather.11.cloned.1.call-done = bf16[2,2048,128]{1,2,0:T(8,128)(2,1)} async-done(((bf16[2,256,128]{1,2,0:T(8,128)(2,1)}), bf16[2,2048,128]{1,2,0:T(8,128)(2,1)}) %all-gather.11.cloned.1.call-update) | async-done | bytes 1048592 | tf_op jit(solution)/shard_map/all_gather | solution.py:81
  673.7 2.7 fusion
  676.4 2.4 fusion.46
  678.9 1.5 collective-permute-done.4
  680.5 1.6 collective-permute-start.5
  682.1 6.8 collective-permute-done.5
  690.8 67.6 %all-reduce.8.cloned.1.call-done = f32[128,128]{1,0:T(8,128)} async-done(((f32[128,128]{1,0:T(8,128)}), f32[128,128]{1,0:T(8,128)}) %all-reduce.8.cloned.1.call-update) | async-done | bytes 65552 | tf_op jit(solution)/shard_map/psum | solution.py:50
  758.4 1.5 select_reduce_fusion
  760.5 1.5 multiply_reduce_fusion
  771.8 1.3 convolution_multiply_fusion
  (160 shorter events, 35.0 us)
Async XLA Ops:
  7.2 88.4 %all-reduce.4.cloned.1.call-start = ((), (), s32[]{:S(2)}) async-start(), calls=%async_computation.4 | async-start | bytes 131072 | tf_op jit(solution)/shard_map/psum | solution.py:50
  7.2 4.2 copy-start
  12.1 1.7 collective-permute-start
  13.9 9.5 %collective-permute-start.1 = (f32[512,128]{1,0:T(8,128)S(1)}, f32[512,128]{1,0:T(8,128)S(1)}, u32[]{:S(2)}, u32[]{:S(2)}) collective-permute-start(f32[512,128]{1,0:T(8,128)S(1)} %add.70), channel_id=1, source_target_pairs={{0,16},{8,24},{16,0},{24,8},{1,17},{9,25},{17,1},{25,9},{2,18},{10... | collective-permute-start | bytes 786440 | tf_op jit(solution)/shard_map/ppermute | solution.py:43
  24.7 158.4 %reduce-scatter.5.cloned.1.call-start = ((), (), s32[]{:S(2)}) async-start(), calls=%async_computation.5 | async-start | bytes 2359296 | tf_op jit(solution)/shard_map/reduce_scatter | solution.py:79
  109.0 2.8 copy-start.1
  113.8 110.3 %all-gather.5.cloned.1.call-start = ((), (), s32[]{:S(2)}) async-start(), calls=%async_computation.6 | async-start | bytes 1179648 | tf_op jit(solution)/shard_map/all_gather | solution.py:81
  184.7 117.2 %reduce-scatter.7.cloned.1.call-start = ((), (), s32[]{:S(2)}) async-start(), calls=%async_computation.7 | async-start | bytes 2359296 | tf_op jit(solution)/shard_map/reduce_scatter | solution.py:79
  233.6 68.4 %copy-start.3 = (f32[2,256,128]{1,2,0:T(8,128)S(1)}, f32[2,256,128]{1,2,0:T(8,128)}, u32[]{:S(2)}) copy-start(f32[2,256,128]{1,2,0:T(8,128)} %reduce-scatter.5.cloned.1.call-done) | copy-start | bytes 786436
  233.6 109.2 %all-gather.7.cloned.1.call-start = ((), (), s32[]{:S(2)}) async-start(), calls=%async_computation.8 | async-start | bytes 1179648 | tf_op jit(solution)/shard_map/all_gather | solution.py:81
  303.7 123.8 %all-reduce.6.cloned.1.call-start = ((), (), s32[]{:S(2)}) async-start(), calls=%async_computation.9 | async-start | bytes 131072 | tf_op jit(solution)/shard_map/psum | solution.py:50
  342.9 2.7 copy-start.5
  348.0 1.6 collective-permute-start.2
  349.6 8.4 %collective-permute-start.3 = (f32[512,128]{0,1:T(8,128)S(1)}, f32[512,128]{0,1:T(8,128)S(1)}, u32[]{:S(2)}, u32[]{:S(2)}) collective-permute-start(f32[512,128]{0,1:T(8,128)S(1)} %add.76), channel_id=1, source_target_pairs={{0,16},{8,24},{16,0},{24,8},{1,17},{9,25},{17,1},{25,9},{2,18},{10... | collective-permute-start | bytes 786440 | tf_op jit(solution)/shard_map/ppermute | solution.py:43
  359.1 155.5 %reduce-scatter.9.cloned.1.call-start = ((), (), s32[]{:S(2)}) async-start(), calls=%async_computation.10 | async-start | bytes 2359296 | tf_op jit(solution)/shard_map/reduce_scatter | solution.py:79
  440.9 2.8 copy-start.2
  445.7 110.0 %all-gather.9.cloned.1.call-start = ((), (), s32[]{:S(2)}) async-start(), calls=%async_computation.11 | async-start | bytes 1179648 | tf_op jit(solution)/shard_map/all_gather | solution.py:81
  516.3 116.5 %reduce-scatter.11.cloned.1.call-start = ((), (), s32[]{:S(2)}) async-start(), calls=%async_computation.12 | async-start | bytes 2359296 | tf_op jit(solution)/shard_map/reduce_scatter | solution.py:79
  564.4 68.4 %copy-start.4 = (f32[2,256,128]{1,2,0:T(8,128)S(1)}, f32[2,256,128]{1,2,0:T(8,128)}, u32[]{:S(2)}) copy-start(f32[2,256,128]{1,2,0:T(8,128)} %reduce-scatter.9.cloned.1.call-done) | copy-start | bytes 786436
  564.4 109.3 %all-gather.11.cloned.1.call-start = ((), (), s32[]{:S(2)}) async-start(), calls=%async_computation.13 | async-start | bytes 1179648 | tf_op jit(solution)/shard_map/all_gather | solution.py:81
  634.5 123.8 %all-reduce.8.cloned.1.call-start = ((), (), s32[]{:S(2)}) async-start(), calls=%async_computation.14 | async-start | bytes 131072 | tf_op jit(solution)/shard_map/psum | solution.py:50
  673.7 2.7 copy-start.6
  678.8 1.6 collective-permute-start.4
  680.5 8.4 %collective-permute-start.5 = (f32[512,128]{0,1:T(8,128)S(1)}, f32[512,128]{0,1:T(8,128)S(1)}, u32[]{:S(2)}, u32[]{:S(2)}) collective-permute-start(f32[512,128]{0,1:T(8,128)S(1)} %add.83), channel_id=1, source_target_pairs={{0,16},{8,24},{16,0},{24,8},{1,17},{9,25},{17,1},{25,9},{2,18},{10... | collective-permute-start | bytes 786440 | tf_op jit(solution)/shard_map/ppermute | solution.py:43
Sparse Core Ops, SparseCore 0:
  24.8 70.7 all-reduce.3
  114.0 69.0 reduce-scatter.4
  185.7 38.4 all-gather.4
  233.7 68.1 reduce-scatter.6
  304.4 38.3 all-gather.6
  359.2 68.2 all-reduce.5
  445.8 68.7 reduce-scatter.8
  517.2 38.3 all-gather.8
  564.5 68.2 reduce-scatter.10
  635.3 38.3 all-gather.10
  690.1 68.2 all-reduce.7
